TPU v7x, 32 devices: a whole 2x2x4 slice. The times are simulated.
32 devices in a mesh: gx: 8 (over z, core), gy: 2 (over x), ga: 2 (over y).
Axes of the slice: x: 2, y: 2, z: 4, core: 2. Of those that a mesh axis runs over, the one named last changes fastest.
Arguments:
- euler_table: float32 [3, 2048], replicated, may hold values from -3.140625 to 3.140625
- crystal: float32 [21], replicated, may hold values from -0.08 to 3.4
- orient: int32 [32, 8, 2, 512], P('ga', 'gx', 'gy'), may hold values from 0 to 2047
- weight: bfloat16 [32, 8, 2, 512], P('ga', 'gx', 'gy'), may hold values from 0.099609375 to 1
- cell_map: int32 [8, 2, 512], P('gx', 'gy'), may hold values from 0 to 511, each once within a row
- density: float32 [64, 8, 16], P('gx', 'gy', 'ga'), may hold values from 0.5 to 2
- velocity: float32 [3, 64, 8, 16], P(None, 'gx', 'gy', 'ga'), may hold values from -6 to 6
- stress: float32 [6, 64, 8, 16], P(None, 'gx', 'gy', 'ga'), may hold values from -6 to 6
Outputs:
- stiffness: float32 [21, 64, 8, 16], P(None, 'gx', 'gy', 'ga')
- final_velocity: float32 [3, 64, 8, 16], P(None, 'gx', 'gy', 'ga')
- final_stress: float32 [6, 64, 8, 16], P(None, 'gx', 'gy', 'ga')
Inputs may be any that keep to these rules, and one draw needn't show every extreme that they name: `cell_map`: each partition's row is a permutation of the 512 canonical indices.
All inputs are finite; a program needn't handle non-finite values.
Results may differ from a plain program's by a relative error of at most 0.0003.
Values sent between devices are 32-bit elements; how exact they have to be, the bound alone decides.
No kernel may reach another device: no remote copies, remote signals or barrier semaphores. Data moves between devices by JAX's collectives and lax.ppermute only.
A program may use at most 128 MiB of HBM per device.

v0:
```python
import jax
import jax.numpy as jnp
from jax import lax
from jax.sharding import PartitionSpec as P

STEPS = 2
stencil_weights = (0.8, -0.2, 4.0 / 105.0, -1.0 / 280.0)
time_step = 0.2
grain_block = 4
voigt_pairs = ((0, 0), (1, 1), (2, 2), (1, 2), (0, 2), (0, 1))
upper_pairs = [
    (row_index, col_index) for row_index in range(6) for col_index in range(row_index, 6)
]


def with_halo(cells, sides, width):
    for axis, dim in sides:
        count = lax.axis_size(axis)
        ends = count - 1
        head = lax.slice_in_dim(cells, 0, width, axis=dim)
        tail = lax.slice_in_dim(cells, cells.shape[dim] - width, cells.shape[dim], axis=dim)
        cells = jnp.concatenate(
            [
                lax.ppermute(tail, axis, [(i, (i + 1) % count) for i in range(ends)]),
                cells,
                lax.ppermute(head, axis, [((i + 1) % count, i) for i in range(ends)]),
            ],
            axis=dim,
        )
    return cells


def symmetric_index(first_index, second_index):
    return upper_pairs.index((min(first_index, second_index), max(first_index, second_index)))


def ordered_sum(summands):
    running = summands[0]
    for summand in summands[1:]:
        running = running + summand
    return running


def rotated_table(euler_table, crystal):
    cos_one, sin_one = (jnp.cos(euler_table[0]), jnp.sin(euler_table[0]))
    cos_mid, sin_mid = (jnp.cos(euler_table[1]), jnp.sin(euler_table[1]))
    cos_two, sin_two = (jnp.cos(euler_table[2]), jnp.sin(euler_table[2]))
    bunge = [
        [
            cos_one * cos_two - sin_one * sin_two * cos_mid,
            sin_one * cos_two + cos_one * sin_two * cos_mid,
            sin_two * sin_mid,
        ],
        [
            -cos_one * sin_two - sin_one * cos_two * cos_mid,
            -sin_one * sin_two + cos_one * cos_two * cos_mid,
            cos_two * sin_mid,
        ],
        [sin_one * sin_mid, -cos_one * sin_mid, cos_mid],
    ]
    rotation = [[bunge[col_index][row_index] for col_index in range(3)] for row_index in range(3)]
    bond = []
    for out_index in range(6):
        first, second = voigt_pairs[out_index]
        bond_row = []
        for in_index in range(6):
            third, fourth = voigt_pairs[in_index]
            if in_index < 3:
                bond_row.append(rotation[first][third] * rotation[second][third])
            else:
                bond_row.append(
                    rotation[first][third] * rotation[second][fourth]
                    + rotation[first][fourth] * rotation[second][third]
                )
        bond.append(bond_row)
    entries = [
        [crystal[symmetric_index(row_index, col_index)] for col_index in range(6)]
        for row_index in range(6)
    ]
    product = [
        [
            ordered_sum([bond[row_index][inner] * entries[inner][col_index] for inner in range(6)])
            for col_index in range(6)
        ]
        for row_index in range(6)
    ]
    rotated = [
        ordered_sum([product[row_index][inner] * bond[col_index][inner] for inner in range(6)])
        for row_index, col_index in upper_pairs
    ]
    return jnp.stack(rotated)


def accumulate(table, orient_rows, weight_rows):
    blocks = orient_rows.shape[0] // grain_block
    count_cells = orient_rows.shape[1]

    def absorb(carry, inputs):
        chosen, masses = inputs
        picked = jnp.take(table, chosen, axis=1)
        masses_wide = masses.astype(jnp.float32)
        return (
            (
                carry[0] + jnp.sum(picked * masses_wide[None], axis=1),
                carry[1] + jnp.sum(masses_wide, axis=0),
            ),
            None,
        )

    initial = (jnp.zeros((21, count_cells), jnp.float32), jnp.zeros((count_cells,), jnp.float32))
    result, unused = lax.scan(
        absorb,
        initial,
        (
            orient_rows.reshape(blocks, grain_block, count_cells),
            weight_rows.reshape(blocks, grain_block, count_cells),
        ),
    )
    return result


def derivative(padded, direction):
    interior = [padded.shape[0]] + [extent - 8 for extent in padded.shape[1:]]

    def window(offset):
        starts = [0, 4, 4, 4]
        starts[direction] = 4 + offset
        return lax.slice(
            padded, starts, [begin + extent for begin, extent in zip(starts, interior)]
        )

    result = stencil_weights[0] * (window(1) - window(-1))
    for order_index in range(1, 4):
        result = result + stencil_weights[order_index] * (
            window(order_index + 1) - window(-order_index - 1)
        )
    return result


def advance_velocity(velocity, padded_stress, density):
    along_x = derivative(jnp.stack([padded_stress[0], padded_stress[5], padded_stress[4]]), 1)
    along_y = derivative(jnp.stack([padded_stress[5], padded_stress[1], padded_stress[3]]), 2)
    along_z = derivative(jnp.stack([padded_stress[4], padded_stress[3], padded_stress[2]]), 3)
    return velocity + time_step * (along_x + along_y + along_z) / density[None]


def advance_stress(stress, padded_velocity, stiffness):
    grad_x = derivative(padded_velocity, 1)
    grad_y = derivative(padded_velocity, 2)
    grad_z = derivative(padded_velocity, 3)
    strain = [
        grad_x[0],
        grad_y[1],
        grad_z[2],
        grad_y[2] + grad_z[1],
        grad_x[2] + grad_z[0],
        grad_x[1] + grad_y[0],
    ]
    updated = []
    for row_index in range(6):
        change = ordered_sum(
            [
                stiffness[symmetric_index(row_index, col_index)] * strain[col_index]
                for col_index in range(6)
            ]
        )
        updated.append(stress[row_index] + time_step * change)
    return jnp.stack(updated)


def on_device(euler_table, crystal, orient, weight, cell_map, density, velocity, stress):
    part_x = lax.axis_size("gx")
    part_y = lax.axis_size("gy")
    layers = lax.axis_size("ga")
    brick_x, brick_y, brick_z = (stress.shape[1], stress.shape[2], stress.shape[3])
    sub_x = brick_x // part_x
    sub_y = brick_y // part_y
    depth = brick_z * layers
    grains = orient.shape[0]
    count_cells = orient.shape[3]
    table = rotated_table(euler_table, crystal)
    summed, total = accumulate(
        table, orient.reshape(grains, count_cells), weight.reshape(grains, count_cells)
    )
    slots = cell_map.reshape(count_cells)
    layer_pos = slots % depth
    remainder = slots // depth
    sub_y_pos = remainder % sub_y
    remainder = remainder // sub_y
    brick_y_pos = remainder % part_y
    remainder = remainder // part_y
    sub_x_pos = remainder % sub_x
    brick_x_pos = remainder // sub_x
    target = (
        ((brick_x_pos * part_y + brick_y_pos) * sub_x + sub_x_pos) * sub_y + sub_y_pos
    ) * depth + layer_pos
    placed = jnp.zeros((21, count_cells), jnp.float32).at[:, target].set(summed)
    counted = jnp.zeros((count_cells,), jnp.float32).at[target].set(total)
    placed = placed.reshape(21, part_x * part_y, sub_x, sub_y, depth)
    counted = counted.reshape(part_x * part_y, sub_x, sub_y, depth)
    placed, counted = (
        lax.psum_scatter(placed, "ga", scatter_dimension=4, tiled=True),
        lax.psum_scatter(counted, "ga", scatter_dimension=3, tiled=True),
    )
    averaged = placed / counted[None]
    moved = lax.all_to_all(averaged, ("gx", "gy"), split_axis=1, concat_axis=1, tiled=True)
    moved = moved.reshape(21, part_x, part_y, sub_x, sub_y, brick_z)
    stiffness = moved.transpose(0, 1, 3, 2, 4, 5).reshape(21, brick_x, brick_y, brick_z)
    for step_index in range(STEPS):
        padded_stress = with_halo(stress, (("gx", 1), ("gy", 2), ("ga", 3)), 4)
        velocity = advance_velocity(velocity, padded_stress, density)
        padded_velocity = with_halo(velocity, (("gx", 1), ("gy", 2), ("ga", 3)), 4)
        stress = advance_stress(stress, padded_velocity, stiffness)
    return (stiffness, velocity, stress)


def solution(mesh):
    return jax.shard_map(
        on_device,
        mesh=mesh,
        in_specs=(
            P(),
            P(),
            P("ga", "gx", "gy", None),
            P("ga", "gx", "gy", None),
            P("gx", "gy", None),
            P("gx", "gy", "ga"),
            P(None, "gx", "gy", "ga"),
            P(None, "gx", "gy", "ga"),
        ),
        out_specs=(P(None, "gx", "gy", "ga"), P(None, "gx", "gy", "ga"), P(None, "gx", "gy", "ga")),
        check_vma=False,
    )
```

profile of v0, /device:TPU:6, one launch (start us, length us, event | category | flops | bytes accessed | tf_op | source)
XLA Modules:
  0.0 305.0 jit_solution(5697528187163204053)
XLA Ops:
  7.2 1.0 copy.84
  8.3 1.7 collective-permute-start
  10.0 1.3 collective-permute-start.1
  12.7 0.8 copy-done.4
  13.4 14.0 %multiply_add_fusion.6 = (f32[1,2048]{1,0:T(1,128)S(1)}, f32[1,2048]{1,0:T(1,128)S(1)}, f32[1,2048]{1,0:T(1,128)S(1)}, f32[1,2048]{1,0:T(1,128)S(1)}, f32[1,2048...) fusion(f32[]{:T(128)} %bitcast.22, f32[]{:T(128)} %bitcast.21, ...), kind=kLoop, calls=%fused_computation.295 | loop fusion | flops 219136 | bytes 131156 | tf_op jit(solution)/shard_map/add | solution.py:40
  27.5 13.8 %multiply_add_fusion.7 = (f32[1,2048]{1,0:T(1,128)S(1)}, f32[1,2048]{1,0:T(1,128)S(1)}, f32[1,2048]{1,0:T(1,128)S(1)}, f32[1,2048]{1,0:T(1,128)S(1)}, f32[1,2048...) fusion(f32[1,2048]{1,0:T(1,128)S(1)} %get-tuple-element.135, ...), kind=kLoop, calls=%fused_computation.296 | loop fusion | flops 186368 | bytes 163924 | tf_op jit(solution)/shard_map/add | solution.py:40
  41.3 13.3 %multiply_add_fusion.34 = (f32[1,2048]{1,0:T(1,128)S(1)}, f32[1,2048]{1,0:T(1,128)S(1)}, f32[1,2048]{1,0:T(1,128)S(1)}, f32[1,2048]{1,0:T(1,128)S(1)}, f32[1,204...) fusion(f32[1,2048]{1,0:T(1,128)S(1)} %get-tuple-element.135, ...), kind=kLoop, calls=%fused_computation.323 | loop fusion | flops 174080 | bytes 155732 | tf_op jit(solution)/shard_map/add | solution.py:40
  54.6 13.5 %multiply_add_fusion.15 = (f32[1,2048]{1,0:T(1,128)S(1)}, f32[1,2048]{1,0:T(1,128)S(1)}, f32[1,2048]{1,0:T(1,128)S(1)}, f32[1,2048]{1,0:T(1,128)S(1)}, f32[1,204...) fusion(f32[1,2048]{1,0:T(1,128)S(1)} %get-tuple-element.135, f32[1,2048]{1,0:T(1,128)S(1)} %get-tuple-element.134, ...), kind=kLoop, calls=%fused_computation.304 | loop fusion | flops 182272 | bytes 155732 | tf_op jit(solution)/shard_map/add | solution.py:40
  68.1 13.5 %multiply_add_fusion.24 = (f32[1,2048]{1,0:T(1,128)S(1)}, f32[1,2048]{1,0:T(1,128)S(1)}, f32[1,2048]{1,0:T(1,128)S(1)}, f32[1,2048]{1,0:T(1,128)S(1)}, f32[1,204...) fusion(f32[1,2048]{1,0:T(1,128)S(1)} %get-tuple-element.135, ...), kind=kLoop, calls=%fused_computation.313 | loop fusion | flops 174080 | bytes 139348 | tf_op jit(solution)/shard_map/add | solution.py:40
  81.7 13.3 %multiply_add_fusion.8 = f32[1,2048]{1,0:T(1,128)S(1)} fusion(f32[1,2048]{1,0:T(1,128)S(1)} %get-tuple-element.148, f32[1,2048]{1,0:T(1,128)S(1)} %get-tuple-element.147, f32[1,2048]{1,0:T(1,128)S(1)} %get-tuple-element.146, f32[1,2048]{1,0:T(1,128)S(1)} %get-tuple-element.145, f32[1,2048]{1,0:T(1,128)S(1)} %get-tuple-element.144, ...), kind=kLoop, calls=%fused_computation.297 | loop fusion | flops 157696 | bytes 57428 | tf_op jit(solution)/shard_map/add | solution.py:40
  95.0 13.3 %multiply_add_fusion.16 = f32[1,2048]{1,0:T(1,128)S(1)} fusion(f32[1,2048]{1,0:T(1,128)S(1)} %get-tuple-element.148, f32[1,2048]{1,0:T(1,128)S(1)} %get-tuple-element.147, f32[1,2048]{1,0:T(1,128)S(1)} %get-tuple-element.146, f32[1,2048]{1,0:T(1,128)S(1)} %get-tuple-element.145, f32[1,2048]{1,0:T(1,128)S(1)} %get-tuple-element.144, ...), kind=kLoop, calls=%fused_computation.305 | loop fusion | flops 157696 | bytes 106580 | tf_op jit(solution)/shard_map/add | solution.py:40
  108.4 13.3 %multiply_add_fusion.45 = (f32[1,2048]{1,0:T(1,128)S(1)}, f32[1,2048]{1,0:T(1,128)S(1)}, f32[1,2048]{1,0:T(1,128)S(1)}, f32[1,2048]{1,0:T(1,128)S(1)}, f32[1,204...) fusion(f32[1,2048]{1,0:T(1,128)S(1)} %get-tuple-element.135, ...), kind=kLoop, calls=%fused_computation.334 | loop fusion | flops 174080 | bytes 155732 | tf_op jit(solution)/shard_map/add | solution.py:40
  122.5 13.3 %multiply_add_fusion.17 = f32[1,2048]{1,0:T(1,128)S(1)} fusion(f32[1,2048]{1,0:T(1,128)S(1)} %get-tuple-element.157, f32[1,2048]{1,0:T(1,128)S(1)} %get-tuple-element.156, f32[1,2048]{1,0:T(1,128)S(1)} %get-tuple-element.155, f32[1,2048]{1,0:T(1,128)S(1)} %get-tuple-element.154, f32[1,2048]{1,0:T(1,128)S(1)} %get-tuple-element.153, ...), kind=kLoop, calls=%fused_computation.306 | loop fusion | flops 157696 | bytes 57428 | tf_op jit(solution)/shard_map/add | solution.py:40
  137.8 1.3 collective-permute-start.2
  139.1 4.6 %collective-permute-start.3 = (f32[6,16,4,8]{1,3,2,0:T(8,128)S(1)}, f32[6,16,4,8]{1,3,2,0:T(8,128)S(1)}, u32[]{:S(2)}, u32[]{:S(2)}) collective-permute-start(f32[6,16,4,8]{1,3,2,0:T(8,128)S(1)} %pad_maximum_fusion.13), channel_id=1, source_target_pairs={{2,0},{3,1},{6,4},{7,5},{10,8},{11,9},{14,12},{15,13},{18,16},{19,... | collective-permute-start | bytes 36872 | tf_op jit(solution)/shard_map/ppermute | solution.py:26
  143.7 25.7 %while.13 = (s32[]{:T(128)}, f32[21,512]{0,1:T(8,128)S(1)}, f32[512]{0:T(512)S(1)}, s32[4,4,512]{2,1,0:T(4,128)S(1)}, f32[21,2048]{0,1:T(8,128)S(1)}, /*index=5*/bf16[4,4,512]{2,1,0:T(4,128)(2,1)S(1)}, s32[]{:T(128)}, s32[]{:T(128)}) while((s32[]{:T(128)}, f32[21,512]{0,1:T(8,128)S(1)}, f32[512]{0:T(512)S(1)}, ...), condition=%wide.region_3.4_spmd.clone, body=%wide.region_0.3_spmd.clone.sunk | while | flops 166915 | bytes 790640 | solution.py:111
  143.7 5.5 %gather_fusion = f32[2048,21]{1,0:T(8,128)S(1)} fusion(f32[21,2048]{0,1:T(8,128)S(1)} %get-tuple-element.310, s32[2048]{0:T(1024)S(1)} %broadcast_clamp_fusion.2), kind=kCustom, calls=%fused_computation.clone.clone.1 | custom fusion | bytes 352256 | tf_op jit(solution)/shard_map/while/body/eval_jaxpr/jit(_take)/gather | solution.py:100
  150.1 5.5 %gather_fusion = f32[2048,21]{1,0:T(8,128)S(1)} fusion(f32[21,2048]{0,1:T(8,128)S(1)} %get-tuple-element.310, s32[2048]{0:T(1024)S(1)} %broadcast_clamp_fusion.2), kind=kCustom, calls=%fused_computation.clone.clone.1 | custom fusion | bytes 352256 | tf_op jit(solution)/shard_map/while/body/eval_jaxpr/jit(_take)/gather | solution.py:100
  156.6 5.5 %gather_fusion = f32[2048,21]{1,0:T(8,128)S(1)} fusion(f32[21,2048]{0,1:T(8,128)S(1)} %get-tuple-element.310, s32[2048]{0:T(1024)S(1)} %broadcast_clamp_fusion.2), kind=kCustom, calls=%fused_computation.clone.clone.1 | custom fusion | bytes 352256 | tf_op jit(solution)/shard_map/while/body/eval_jaxpr/jit(_take)/gather | solution.py:100
  163.0 5.5 %gather_fusion = f32[2048,21]{1,0:T(8,128)S(1)} fusion(f32[21,2048]{0,1:T(8,128)S(1)} %get-tuple-element.310, s32[2048]{0:T(1024)S(1)} %broadcast_clamp_fusion.2), kind=kCustom, calls=%fused_computation.clone.clone.1 | custom fusion | bytes 352256 | tf_op jit(solution)/shard_map/while/body/eval_jaxpr/jit(_take)/gather | solution.py:100
  169.6 1.3 collective-permute-start.4
  170.9 4.6 %collective-permute-start.5 = (f32[6,16,12,4]{1,3,2,0:T(4,128)S(1)}, f32[6,16,12,4]{1,3,2,0:T(4,128)S(1)}, u32[]{:S(2)}, u32[]{:S(2)}) collective-permute-start(f32[6,16,12,4]{1,3,2,0:T(4,128)S(1)} %get-tuple-element.205), channel_id=1, source_target_pairs={{1,0},{3,2},{5,4},{7,6},{9,8},{11,10},{13,12},{15,14},{17,16},{19,... | collective-permute-start | bytes 55304 | tf_op jit(solution)/shard_map/ppermute | solution.py:26
  175.5 1.8 scatter_custom_fusion
  177.3 0.8 copy.81
  178.2 2.4 scatter_custom_fusion.1
  182.7 6.7 %all-reduce = f32[16,1,2,16]{0,2,1,3:T(2,128)S(1)} all-reduce(f32[16,1,2,16]{0,2,1,3:T(2,128)S(1)} %copy.82), channel_id=3, replica_groups=mesh['gx'=8,'gy'=2,'ga'=2] {'ga'}, use_global_device_ids=true, to_apply=%region_7.8.clone | all-reduce | flops 512 | bytes 4096
  193.0 1.3 collective-permute-start.6
  194.3 3.0 collective-permute-start.7
  197.3 0.8 collective-permute-done.7
  198.2 1.3 collective-permute-start.8
  199.5 1.3 collective-permute-start.9
  200.8 0.8 collective-permute-done.8
  201.7 4.3 %collective-permute-done.9 = f32[3,16,4,8]{3,2,1,0:T(4,128)S(1)} collective-permute-done((f32[3,16,4,8]{3,2,1,0:T(4,128)S(1)}, f32[3,16,4,8]{3,2,1,0:T(4,128)S(1)}, u32[]{:S(2)}, u32[]{:S(2)}) %collective-permute-start.9) | collective-permute-done | bytes 6176 | tf_op jit(solution)/shard_map/ppermute | solution.py:24
  206.2 3.9 %collective-permute-start.10 = (f32[3,16,12,4]{3,2,1,0:T(8,128)S(1)}, f32[3,16,12,4]{3,2,1,0:T(8,128)S(1)}, u32[]{:S(2)}, u32[]{:S(2)}) collective-permute-start(f32[3,16,12,4]{3,2,1,0:T(8,128)S(1)} %get-tuple-element.202), channel_id=1, source_target_pairs={{1,0},{3,2},{5,4},{7,6},{9,8},{11,10},{13,12},{15,14},{17,16},{19,... | collective-permute-start | bytes 27656 | tf_op jit(solution)/shard_map/ppermute | solution.py:26
  210.1 1.3 collective-permute-start.11
  211.6 1.0 broadcast_divide_fusion
  212.7 0.7 reshape.481
  213.5 11.0 %all-to-all-start = ((f32[16,1,336]{2,1,0:T(1,128)}), f32[16,1,336]{2,1,0:T(1,128)S(1)}, u32[]{:S(2)}, u32[]{:S(2)}) async-start(f32[16,1,336]{2,1,0:T(1,128)} %reshape.481), calls=%async_computation.1 | async-start | bytes 49152 | tf_op jit(solution)/shard_map/all_to_all | solution.py:206
  224.5 0.9 fusion.78
  225.3 4.2 %all-to-all-done = f32[16,1,336]{2,1,0:T(1,128)S(1)} async-done(((f32[16,1,336]{2,1,0:T(1,128)}), f32[16,1,336]{2,1,0:T(1,128)S(1)}, u32[]{:S(2)}, u32[]{:S(2)}) %all-to-all-start) | async-done | bytes 21536 | tf_op jit(solution)/shard_map/all_to_all | solution.py:206
  230.9 1.7 slice_reduce_fusion
  233.8 2.0 collective-permute-start.12
  235.8 1.3 collective-permute-start.13
  237.1 1.9 collective-permute-done.13
  239.1 1.3 collective-permute-start.14
  240.4 4.6 %collective-permute-start.15 = (f32[6,16,4,8]{3,2,1,0:T(4,128)S(1)}, f32[6,16,4,8]{3,2,1,0:T(4,128)S(1)}, u32[]{:S(2)}, u32[]{:S(2)}) collective-permute-start(f32[6,16,4,8]{3,2,1,0:T(4,128)S(1)} %pad_maximum_fusion.12), channel_id=1, source_target_pairs={{2,0},{3,1},{6,4},{7,5},{10,8},{11,9},{14,12},{15,13},{18,16},{19,... | collective-permute-start | bytes 36872 | tf_op jit(solution)/shard_map/ppermute | solution.py:26
  245.0 2.0 collective-permute-done.14
  246.9 1.7 collective-permute-done.15
  249.7 1.3 collective-permute-start.16
  251.5 4.6 %collective-permute-start.17 = (f32[6,16,12,4]{1,3,2,0:T(4,128)S(1)}, f32[6,16,12,4]{1,3,2,0:T(4,128)S(1)}, u32[]{:S(2)}, u32[]{:S(2)}) collective-permute-start(f32[6,16,12,4]{1,3,2,0:T(4,128)S(1)} %copy.91), channel_id=1, source_target_pairs={{1,0},{3,2},{5,4},{7,6},{9,8},{11,10},{13,12},{15,14},{17,16},{19,... | collective-permute-start | bytes 55304 | tf_op jit(solution)/shard_map/ppermute | solution.py:26
  256.1 1.3 collective-permute-done.16
  257.9 1.7 collective-permute-done.17
  261.7 1.3 collective-permute-start.18
  263.0 3.3 %collective-permute-start.19 = (f32[3,4,4,8]{3,2,1,0:T(4,128)S(1)}, f32[3,4,4,8]{3,2,1,0:T(4,128)S(1)}, u32[]{:S(2)}, u32[]{:S(2)}) collective-permute-start(f32[3,4,4,8]{3,2,1,0:T(4,128)S(1)} %get-tuple-element.218), channel_id=1, source_target_pairs={{0,4},{4,8},{8,12},{12,16},{16,20},{20,24},{24,28},{1,5},{5,9},{9,... | collective-permute-start | bytes 4616 | tf_op jit(solution)/shard_map/ppermute | solution.py:24
  266.3 0.8 collective-permute-done.19
  267.2 4.4 %collective-permute-start.20 = (f32[3,16,4,8]{3,2,1,0:T(4,128)S(1)}, f32[3,16,4,8]{3,2,1,0:T(4,128)S(1)}, u32[]{:S(2)}, u32[]{:S(2)}) collective-permute-start(f32[3,16,4,8]{3,2,1,0:T(4,128)S(1)} %pad_maximum_fusion.15), channel_id=1, source_target_pairs={{2,0},{3,1},{6,4},{7,5},{10,8},{11,9},{14,12},{15,13},{18,16},{19,... | collective-permute-start | bytes 18440 | tf_op jit(solution)/shard_map/ppermute | solution.py:26
  271.6 1.3 collective-permute-start.21
  272.9 0.8 collective-permute-done.20
  273.8 4.3 %collective-permute-done.21 = f32[3,16,4,8]{3,2,1,0:T(4,128)S(1)} collective-permute-done((f32[3,16,4,8]{3,2,1,0:T(4,128)S(1)}, f32[3,16,4,8]{3,2,1,0:T(4,128)S(1)}, u32[]{:S(2)}, u32[]{:S(2)}) %collective-permute-start.21) | collective-permute-done | bytes 6176 | tf_op jit(solution)/shard_map/ppermute | solution.py:24
  278.4 4.4 %collective-permute-start.22 = (f32[3,16,12,4]{3,2,1,0:T(8,128)S(1)}, f32[3,16,12,4]{3,2,1,0:T(8,128)S(1)}, u32[]{:S(2)}, u32[]{:S(2)}) collective-permute-start(f32[3,16,12,4]{3,2,1,0:T(8,128)S(1)} %get-tuple-element.200), channel_id=1, source_target_pairs={{1,0},{3,2},{5,4},{7,6},{9,8},{11,10},{13,12},{15,14},{17,16},{19,... | collective-permute-start | bytes 27656 | tf_op jit(solution)/shard_map/ppermute | solution.py:26
  282.8 1.3 collective-permute-start.23
  284.2 8.0 %collective-permute-done.22 = f32[3,16,12,4]{3,2,1,0:T(8,128)S(1)} collective-permute-done((f32[3,16,12,4]{3,2,1,0:T(8,128)S(1)}, f32[3,16,12,4]{3,2,1,0:T(8,128)S(1)}, u32[]{:S(2)}, u32[]{:S(2)}) %collective-permute-start.22) | collective-permute-done | bytes 9248 | tf_op jit(solution)/shard_map/ppermute | solution.py:26
  292.2 4.1 %collective-permute-done.23 = f32[3,16,12,4]{3,2,1,0:T(8,128)S(1)} collective-permute-done((f32[3,16,12,4]{3,2,1,0:T(8,128)S(1)}, f32[3,16,12,4]{3,2,1,0:T(8,128)S(1)}, u32[]{:S(2)}, u32[]{:S(2)}) %collective-permute-start.23) | collective-permute-done | bytes 9248 | tf_op jit(solution)/shard_map/ppermute | solution.py:24
  296.4 0.9 fusion.36
  (145 shorter events, 21.5 us)
Async XLA Ops:
  7.2 204.5 %reduce-scatter.2.cloned.1.call-start = ((), (), s32[]{:S(2)}) async-start(), calls=%async_computation.2 | async-start | bytes 393216 | tf_op jit(solution)/shard_map/reduce_scatter | solution.py:202
  8.3 3.1 %copy-start.3 = (f32[21]{0:T(128)S(1)}, f32[21]{0:T(128)}, u32[]{:S(2)}) copy-start(f32[21]{0:T(128)} %param.11) | copy-start | bytes 256
  8.3 129.4 %collective-permute-start = (f32[6,4,4,8]{1,3,2,0:T(8,128)S(1)}, f32[6,4,4,8]{1,3,2,0:T(8,128)S(1)}, u32[]{:S(2)}, u32[]{:S(2)}) collective-permute-start(f32[6,4,4,8]{1,3,2,0:T(8,128)S(1)} %get-tuple-element.214), channel_id=1, source_target_pairs={{0,4},{4,8},{8,12},{12,16},{16,20},{20,24},{24,28},{1,5},{5,9},{9,... | collective-permute-start | bytes 9224 | tf_op jit(solution)/shard_map/ppermute | solution.py:24
  10.0 127.6 %collective-permute-start.1 = (f32[6,4,4,8]{1,3,2,0:T(8,128)S(1)}, f32[6,4,4,8]{1,3,2,0:T(8,128)S(1)}, u32[]{:S(2)}, u32[]{:S(2)}) collective-permute-start(f32[6,4,4,8]{1,3,2,0:T(8,128)S(1)} %get-tuple-element.215), channel_id=1, source_target_pairs={{4,0},{8,4},{12,8},{16,12},{20,16},{24,20},{28,24},{5,1},{9,5},{13... | collective-permute-start | bytes 9224 | tf_op jit(solution)/shard_map/ppermute | solution.py:26
  12.7 0.8 copy-start.4
  136.1 0.8 copy-start.7
  136.9 0.7 copy-start.8
  137.8 31.6 %collective-permute-start.2 = (f32[6,16,4,8]{1,3,2,0:T(8,128)S(1)}, f32[6,16,4,8]{1,3,2,0:T(8,128)S(1)}, u32[]{:S(2)}, u32[]{:S(2)}) collective-permute-start(f32[6,16,4,8]{1,3,2,0:T(8,128)S(1)} %pad_maximum_fusion.13), channel_id=1, source_target_pairs={{0,2},{1,3},{4,6},{5,7},{8,10},{9,11},{12,14},{13,15},{16,18},{17,... | collective-permute-start | bytes 36872 | tf_op jit(solution)/shard_map/ppermute | solution.py:24
  139.1 30.3 %collective-permute-start.3 = (f32[6,16,4,8]{1,3,2,0:T(8,128)S(1)}, f32[6,16,4,8]{1,3,2,0:T(8,128)S(1)}, u32[]{:S(2)}, u32[]{:S(2)}) collective-permute-start(f32[6,16,4,8]{1,3,2,0:T(8,128)S(1)} %pad_maximum_fusion.13), channel_id=1, source_target_pairs={{2,0},{3,1},{6,4},{7,5},{10,8},{11,9},{14,12},{15,13},{18,16},{19,... | collective-permute-start | bytes 36872 | tf_op jit(solution)/shard_map/ppermute | solution.py:26
  169.6 5.9 %copy-start.10 = (s32[1,1,512]{2,1,0:T(1,128)S(1)}, s32[1,1,512]{2,1,0:T(1,128)}, u32[]{:S(2)}) copy-start(s32[1,1,512]{2,1,0:T(1,128)} %param.14) | copy-start | bytes 6148
  169.6 20.3 %collective-permute-start.4 = (f32[6,16,12,4]{1,3,2,0:T(4,128)S(1)}, f32[6,16,12,4]{1,3,2,0:T(4,128)S(1)}, u32[]{:S(2)}, u32[]{:S(2)}) collective-permute-start(f32[6,16,12,4]{1,3,2,0:T(4,128)S(1)} %get-tuple-element.204), channel_id=1, source_target_pairs={{0,1},{2,3},{4,5},{6,7},{8,9},{10,11},{12,13},{14,15},{16,17},{18,... | collective-permute-start | bytes 55304 | tf_op jit(solution)/shard_map/ppermute | solution.py:24
  170.9 19.5 %collective-permute-start.5 = (f32[6,16,12,4]{1,3,2,0:T(4,128)S(1)}, f32[6,16,12,4]{1,3,2,0:T(4,128)S(1)}, u32[]{:S(2)}, u32[]{:S(2)}) collective-permute-start(f32[6,16,12,4]{1,3,2,0:T(4,128)S(1)} %get-tuple-element.205), channel_id=1, source_target_pairs={{1,0},{3,2},{5,4},{7,6},{9,8},{11,10},{13,12},{15,14},{17,16},{19,... | collective-permute-start | bytes 55304 | tf_op jit(solution)/shard_map/ppermute | solution.py:26
  180.8 0.7 copy-start.11
  191.5 0.7 copy-start.5
  191.5 0.8 copy-start.6
  193.0 4.4 %collective-permute-start.6 = (f32[3,4,4,8]{3,2,1,0:T(4,128)S(1)}, f32[3,4,4,8]{3,2,1,0:T(4,128)S(1)}, u32[]{:S(2)}, u32[]{:S(2)}) collective-permute-start(f32[3,4,4,8]{3,2,1,0:T(4,128)S(1)} %get-tuple-element.221), channel_id=1, source_target_pairs={{4,0},{8,4},{12,8},{16,12},{20,16},{24,20},{28,24},{5,1},{9,5},{13... | collective-permute-start | bytes 4616 | tf_op jit(solution)/shard_map/ppermute | solution.py:26
  194.3 3.9 %collective-permute-start.7 = (f32[3,4,4,8]{3,2,1,0:T(4,128)S(1)}, f32[3,4,4,8]{3,2,1,0:T(4,128)S(1)}, u32[]{:S(2)}, u32[]{:S(2)}) collective-permute-start(f32[3,4,4,8]{3,2,1,0:T(4,128)S(1)} %get-tuple-element.220), channel_id=1, source_target_pairs={{0,4},{4,8},{8,12},{12,16},{16,20},{20,24},{24,28},{1,5},{5,9},{9,... | collective-permute-start | bytes 4616 | tf_op jit(solution)/shard_map/ppermute | solution.py:24
  198.2 3.5 %collective-permute-start.8 = (f32[3,16,4,8]{3,2,1,0:T(4,128)S(1)}, f32[3,16,4,8]{3,2,1,0:T(4,128)S(1)}, u32[]{:S(2)}, u32[]{:S(2)}) collective-permute-start(f32[3,16,4,8]{3,2,1,0:T(4,128)S(1)} %pad_maximum_fusion.14), channel_id=1, source_target_pairs={{2,0},{3,1},{6,4},{7,5},{10,8},{11,9},{14,12},{15,13},{18,16},{19,... | collective-permute-start | bytes 18440 | tf_op jit(solution)/shard_map/ppermute | solution.py:26
  199.5 6.5 %collective-permute-start.9 = (f32[3,16,4,8]{3,2,1,0:T(4,128)S(1)}, f32[3,16,4,8]{3,2,1,0:T(4,128)S(1)}, u32[]{:S(2)}, u32[]{:S(2)}) collective-permute-start(f32[3,16,4,8]{3,2,1,0:T(4,128)S(1)} %pad_maximum_fusion.14), channel_id=1, source_target_pairs={{0,2},{1,3},{4,6},{5,7},{8,10},{9,11},{12,14},{13,15},{16,18},{17,... | collective-permute-start | bytes 18440 | tf_op jit(solution)/shard_map/ppermute | solution.py:24
  206.2 18.2 %collective-permute-start.10 = (f32[3,16,12,4]{3,2,1,0:T(8,128)S(1)}, f32[3,16,12,4]{3,2,1,0:T(8,128)S(1)}, u32[]{:S(2)}, u32[]{:S(2)}) collective-permute-start(f32[3,16,12,4]{3,2,1,0:T(8,128)S(1)} %get-tuple-element.202), channel_id=1, source_target_pairs={{1,0},{3,2},{5,4},{7,6},{9,8},{11,10},{13,12},{15,14},{17,16},{19,... | collective-permute-start | bytes 27656 | tf_op jit(solution)/shard_map/ppermute | solution.py:26
  210.1 14.3 %collective-permute-start.11 = (f32[3,16,12,4]{3,2,1,0:T(8,128)S(1)}, f32[3,16,12,4]{3,2,1,0:T(8,128)S(1)}, u32[]{:S(2)}, u32[]{:S(2)}) collective-permute-start(f32[3,16,12,4]{3,2,1,0:T(8,128)S(1)} %get-tuple-element.203), channel_id=1, source_target_pairs={{0,1},{2,3},{4,5},{6,7},{8,9},{10,11},{12,13},{14,15},{16,17},{18,... | collective-permute-start | bytes 27656 | tf_op jit(solution)/shard_map/ppermute | solution.py:24
  213.5 16.1 %all-to-all-start = ((f32[16,1,336]{2,1,0:T(1,128)}), f32[16,1,336]{2,1,0:T(1,128)S(1)}, u32[]{:S(2)}, u32[]{:S(2)}) async-start(f32[16,1,336]{2,1,0:T(1,128)} %reshape.481), calls=%async_computation.1 | async-start | bytes 49152 | tf_op jit(solution)/shard_map/all_to_all | solution.py:206
  230.9 1.7 copy-start
  232.6 0.9 copy-start.2
  233.8 3.3 %collective-permute-start.12 = (f32[6,4,4,8]{3,2,1,0:T(4,128)S(1)}, f32[6,4,4,8]{3,2,1,0:T(4,128)S(1)}, u32[]{:S(2)}, u32[]{:S(2)}) collective-permute-start(f32[6,4,4,8]{3,2,1,0:T(4,128)S(1)} %get-tuple-element.212), channel_id=1, source_target_pairs={{0,4},{4,8},{8,12},{12,16},{16,20},{20,24},{24,28},{1,5},{5,9},{9,... | collective-permute-start | bytes 9224 | tf_op jit(solution)/shard_map/ppermute | solution.py:24
  235.8 3.2 %collective-permute-start.13 = (f32[6,4,4,8]{3,2,1,0:T(4,128)S(1)}, f32[6,4,4,8]{3,2,1,0:T(4,128)S(1)}, u32[]{:S(2)}, u32[]{:S(2)}) collective-permute-start(f32[6,4,4,8]{3,2,1,0:T(4,128)S(1)} %get-tuple-element.213), channel_id=1, source_target_pairs={{4,0},{8,4},{12,8},{16,12},{20,16},{24,20},{28,24},{5,1},{9,5},{13... | collective-permute-start | bytes 9224 | tf_op jit(solution)/shard_map/ppermute | solution.py:26
  239.1 7.9 %collective-permute-start.14 = (f32[6,16,4,8]{3,2,1,0:T(4,128)S(1)}, f32[6,16,4,8]{3,2,1,0:T(4,128)S(1)}, u32[]{:S(2)}, u32[]{:S(2)}) collective-permute-start(f32[6,16,4,8]{3,2,1,0:T(4,128)S(1)} %pad_maximum_fusion.12), channel_id=1, source_target_pairs={{0,2},{1,3},{4,6},{5,7},{8,10},{9,11},{12,14},{13,15},{16,18},{17,... | collective-permute-start | bytes 36872 | tf_op jit(solution)/shard_map/ppermute | solution.py:24
  240.4 8.3 %collective-permute-start.15 = (f32[6,16,4,8]{3,2,1,0:T(4,128)S(1)}, f32[6,16,4,8]{3,2,1,0:T(4,128)S(1)}, u32[]{:S(2)}, u32[]{:S(2)}) collective-permute-start(f32[6,16,4,8]{3,2,1,0:T(4,128)S(1)} %pad_maximum_fusion.12), channel_id=1, source_target_pairs={{2,0},{3,1},{6,4},{7,5},{10,8},{11,9},{14,12},{15,13},{18,16},{19,... | collective-permute-start | bytes 36872 | tf_op jit(solution)/shard_map/ppermute | solution.py:26
  249.7 7.7 %collective-permute-start.16 = (f32[6,16,12,4]{1,3,2,0:T(4,128)S(1)}, f32[6,16,12,4]{1,3,2,0:T(4,128)S(1)}, u32[]{:S(2)}, u32[]{:S(2)}) collective-permute-start(f32[6,16,12,4]{1,3,2,0:T(4,128)S(1)} %copy.90), channel_id=1, source_target_pairs={{0,1},{2,3},{4,5},{6,7},{8,9},{10,11},{12,13},{14,15},{16,17},{18,... | collective-permute-start | bytes 55304 | tf_op jit(solution)/shard_map/ppermute | solution.py:24
  251.5 8.1 %collective-permute-start.17 = (f32[6,16,12,4]{1,3,2,0:T(4,128)S(1)}, f32[6,16,12,4]{1,3,2,0:T(4,128)S(1)}, u32[]{:S(2)}, u32[]{:S(2)}) collective-permute-start(f32[6,16,12,4]{1,3,2,0:T(4,128)S(1)} %copy.91), channel_id=1, source_target_pairs={{1,0},{3,2},{5,4},{7,6},{9,8},{11,10},{13,12},{15,14},{17,16},{19,... | collective-permute-start | bytes 55304 | tf_op jit(solution)/shard_map/ppermute | solution.py:26
  261.7 34.7 %copy-start.1 = (f32[3,8,4,8]{3,2,1,0:T(4,128)}, f32[3,8,4,8]{3,2,1,0:T(4,128)S(1)}, u32[]{:S(2)}) copy-start(f32[3,8,4,8]{3,2,1,0:T(4,128)S(1)} %divide_add_fusion) | copy-start | bytes 9220
  261.7 4.6 %collective-permute-start.18 = (f32[3,4,4,8]{3,2,1,0:T(4,128)S(1)}, f32[3,4,4,8]{3,2,1,0:T(4,128)S(1)}, u32[]{:S(2)}, u32[]{:S(2)}) collective-permute-start(f32[3,4,4,8]{3,2,1,0:T(4,128)S(1)} %get-tuple-element.219), channel_id=1, source_target_pairs={{4,0},{8,4},{12,8},{16,12},{20,16},{24,20},{28,24},{5,1},{9,5},{13... | collective-permute-start | bytes 4616 | tf_op jit(solution)/shard_map/ppermute | solution.py:26
  263.0 4.2 %collective-permute-start.19 = (f32[3,4,4,8]{3,2,1,0:T(4,128)S(1)}, f32[3,4,4,8]{3,2,1,0:T(4,128)S(1)}, u32[]{:S(2)}, u32[]{:S(2)}) collective-permute-start(f32[3,4,4,8]{3,2,1,0:T(4,128)S(1)} %get-tuple-element.218), channel_id=1, source_target_pairs={{0,4},{4,8},{8,12},{12,16},{16,20},{20,24},{24,28},{1,5},{5,9},{9,... | collective-permute-start | bytes 4616 | tf_op jit(solution)/shard_map/ppermute | solution.py:24
  267.2 6.6 %collective-permute-start.20 = (f32[3,16,4,8]{3,2,1,0:T(4,128)S(1)}, f32[3,16,4,8]{3,2,1,0:T(4,128)S(1)}, u32[]{:S(2)}, u32[]{:S(2)}) collective-permute-start(f32[3,16,4,8]{3,2,1,0:T(4,128)S(1)} %pad_maximum_fusion.15), channel_id=1, source_target_pairs={{2,0},{3,1},{6,4},{7,5},{10,8},{11,9},{14,12},{15,13},{18,16},{19,... | collective-permute-start | bytes 18440 | tf_op jit(solution)/shard_map/ppermute | solution.py:26
  271.6 6.5 %collective-permute-start.21 = (f32[3,16,4,8]{3,2,1,0:T(4,128)S(1)}, f32[3,16,4,8]{3,2,1,0:T(4,128)S(1)}, u32[]{:S(2)}, u32[]{:S(2)}) collective-permute-start(f32[3,16,4,8]{3,2,1,0:T(4,128)S(1)} %pad_maximum_fusion.15), channel_id=1, source_target_pairs={{0,2},{1,3},{4,6},{5,7},{8,10},{9,11},{12,14},{13,15},{16,18},{17,... | collective-permute-start | bytes 18440 | tf_op jit(solution)/shard_map/ppermute | solution.py:24
  278.4 13.9 %collective-permute-start.22 = (f32[3,16,12,4]{3,2,1,0:T(8,128)S(1)}, f32[3,16,12,4]{3,2,1,0:T(8,128)S(1)}, u32[]{:S(2)}, u32[]{:S(2)}) collective-permute-start(f32[3,16,12,4]{3,2,1,0:T(8,128)S(1)} %get-tuple-element.200), channel_id=1, source_target_pairs={{1,0},{3,2},{5,4},{7,6},{9,8},{11,10},{13,12},{15,14},{17,16},{19,... | collective-permute-start | bytes 27656 | tf_op jit(solution)/shard_map/ppermute | solution.py:26
  282.8 13.6 %collective-permute-start.23 = (f32[3,16,12,4]{3,2,1,0:T(8,128)S(1)}, f32[3,16,12,4]{3,2,1,0:T(8,128)S(1)}, u32[]{:S(2)}, u32[]{:S(2)}) collective-permute-start(f32[3,16,12,4]{3,2,1,0:T(8,128)S(1)} %get-tuple-element.201), channel_id=1, source_target_pairs={{0,1},{2,3},{4,5},{6,7},{8,9},{10,11},{12,13},{14,15},{16,17},{18,... | collective-permute-start | bytes 27656 | tf_op jit(solution)/shard_map/ppermute | solution.py:24
  297.5 0.6 copy-start.9
Sparse Core Ops, SparseCore 0:
  178.3 14.7 reduce-scatter.1
where the time goes:
time: 308 us; the launch traced here: 305 us
  other arithmetic  134 us (44%)
  starting transfers between devices  68.9 us (22%)
  local copies, waits for them, and re-layouts  43 us (14%)
  waiting for transfers between devices  37 us (12%)
  between operations  15.5 us (5%)
  blocking collectives  6.73 us (2%)
    add x15, other arithmetic, ordered_sum(): running = running + summand  122 us
    ppermute x12, starting transfers between devices, with_halo(): lax.ppermute(head, axis, [((i + 1) % count, i) for i in range(ends)])  37.4 us
    gather x4, local copies, waits for them, and re-layouts, absorb(): picked = jnp.take(table, chosen, axis=1)  21.9 us
    ppermute x12, starting transfers between devices, with_halo(): lax.ppermute(tail, axis, [(i, (i + 1) % count) for i in range(ends)])  20.5 us
    ppermute x12, waiting for transfers between devices, with_halo(): lax.ppermute(tail, axis, [(i, (i + 1) % count) for i in range(ends)])  17.7 us
    ppermute x12, waiting for transfers between devices, with_halo(): lax.ppermute(head, axis, [((i + 1) % count, i) for i in range(ends)])  15.1 us
    all_to_all x1, starting transfers between devices, on_device(): lax.all_to_all(averaged, ('gx', 'gy'), split_axis=1, concat_axis=1, tiled...  11 us
    unnamed x29, local copies, waits for them, and re-layouts  7.27 us
  transfers between devices with their start and end apart: 26, of which 14 were waited for; matrix products, arithmetic and copies ran while one was open for 53% of the time, Pallas kernels for 0%

commit v1 on v0

--- a/solution.py
+++ b/solution.py
@@ -11,6 +11,18 @@
 upper_pairs = [
     (row_index, col_index) for row_index in range(6) for col_index in range(row_index, 6)
 ]
+
+
+def in_blocks(x, dim, size):
+    shape = x.shape
+    blocks = x.reshape(*shape[:dim], size, shape[dim] // size, *shape[dim + 1 :])
+    return jnp.moveaxis(blocks, dim, 0)
+
+
+def joined_along(parts, dim):
+    dims = list(parts.shape[1:])
+    dims[dim] *= parts.shape[0]
+    return jnp.moveaxis(parts, 0, dim).reshape(dims)
 
 
 def with_halo(cells, sides, width):
@@ -203,7 +215,18 @@
         lax.psum_scatter(counted, "ga", scatter_dimension=3, tiled=True),
     )
     averaged = placed / counted[None]
-    moved = lax.all_to_all(averaged, ("gx", "gy"), split_axis=1, concat_axis=1, tiled=True)
+    devices, index = (lax.axis_size(("gx", "gy")), lax.axis_index(("gx", "gy")))
+    parts = in_blocks(averaged, 1, devices)
+    finished = [parts[index]]
+    for turn in range(1, devices):
+        sent = parts[(index + turn) % devices]
+        finished.append(
+            lax.ppermute(
+                sent, ("gx", "gy"), [(i_2, (i_2 + turn) % devices) for i_2 in range(devices)]
+            )
+        )
+    parts = jnp.stack(finished)[(index - jnp.arange(devices)) % devices]
+    moved = joined_along(parts, 1)
     moved = moved.reshape(21, part_x, part_y, sub_x, sub_y, brick_z)
     stiffness = moved.transpose(0, 1, 3, 2, 4, 5).reshape(21, brick_x, brick_y, brick_z)
     for step_index in range(STEPS):

time: 308 us -> 334 us (1.084)
  starting transfers between devices: 68.9 us -> 84 us
  waiting for transfers between devices: 37 us -> 49.4 us
    ppermute x0 -> x15, starting transfers between devices: none -> 23 us  [on_device(): lax.ppermute(sent, ('gx', 'gy'), [(i_2, (i_2 + turn) % devices) for i_2 i...]
    all_to_all x1 -> x0, starting transfers between devices: 11 us -> none  [on_device(): lax.all_to_all(averaged, ('gx', 'gy'), split_axis=1, concat_axis=1, tiled...]
    ppermute x12, waiting for transfers between devices: 15.1 us -> 23.5 us  [with_halo(): lax.ppermute(head, axis, [((i + 1) % count, i) for i in range(ends)])]
    ppermute x12, waiting for transfers between devices: 17.7 us -> 24.5 us  [with_halo(): lax.ppermute(tail, axis, [(i, (i + 1) % count) for i in range(ends)])]
    all_to_all x1 -> x0, waiting for transfers between devices: 4.25 us -> none  [on_device(): lax.all_to_all(averaged, ('gx', 'gy'), split_axis=1, concat_axis=1, tiled...]
    ppermute x12, starting transfers between devices: 37.4 us -> 41.5 us  [with_halo(): lax.ppermute(head, axis, [((i + 1) % count, i) for i in range(ends)])]
    unnamed x29 -> x42, local copies, waits for them, and re-layouts: 7.27 us -> 6.44 us
  transfers between devices with their start and end apart: 26 -> 40, of which waited for: 14 -> 20; matrix products, arithmetic and copies ran while one was open for 53% -> 49% of each run, Pallas kernels for 0% -> 0%
where the time goes in v1:
time: 334 us; the launch traced here: 332 us
  other arithmetic  133 us (40%)
  starting transfers between devices  84 us (25%)
  waiting for transfers between devices  49.4 us (15%)
  local copies, waits for them, and re-layouts  42 us (13%)
  between operations  15.7 us (5%)
  blocking collectives  7.16 us (2%)
    add x15, other arithmetic, ordered_sum(): running = running + summand  122 us
    ppermute x12, starting transfers between devices, with_halo(): lax.ppermute(head, axis, [((i + 1) % count, i) for i in range(ends)])  41.5 us
    ppermute x12, waiting for transfers between devices, with_halo(): lax.ppermute(tail, axis, [(i, (i + 1) % count) for i in range(ends)])  24.5 us
    ppermute x12, waiting for transfers between devices, with_halo(): lax.ppermute(head, axis, [((i + 1) % count, i) for i in range(ends)])  23.5 us
    ppermute x15, starting transfers between devices, on_device(): lax.ppermute(sent, ('gx', 'gy'), [(i_2, (i_2 + turn) % devices) for i_2 i...  23 us
    gather x4, local copies, waits for them, and re-layouts, absorb(): picked = jnp.take(table, chosen, axis=1)  21.9 us
    ppermute x12, starting transfers between devices, with_halo(): lax.ppermute(tail, axis, [(i, (i + 1) % count) for i in range(ends)])  19.5 us
    unnamed x1, blocking collectives  7.16 us
  transfers between devices with their start and end apart: 40, of which 20 were waited for; matrix products, arithmetic and copies ran while one was open for 49% of the time, Pallas kernels for 0%

profile of v1, /device:TPU:6, one launch (start us, length us, event | category | flops | bytes accessed | tf_op | source)
XLA Modules:
  0.0 331.6 jit_solution(9157314191996244677)
XLA Ops:
  8.3 1.7 collective-permute-start.15
  10.0 1.3 collective-permute-start.16
  13.4 14.1 %multiply_add_fusion.6 = (f32[1,2048]{1,0:T(1,128)S(1)}, f32[1,2048]{1,0:T(1,128)S(1)}, f32[1,2048]{1,0:T(1,128)S(1)}, f32[1,2048]{1,0:T(1,128)S(1)}, f32[1,2048...) fusion(f32[]{:T(128)} %bitcast.22, f32[]{:T(128)} %bitcast.21, ...), kind=kLoop, calls=%fused_computation.312 | loop fusion | flops 219136 | bytes 131156 | tf_op jit(solution)/shard_map/add | solution.py:52
  27.5 13.8 %multiply_add_fusion.7 = (f32[1,2048]{1,0:T(1,128)S(1)}, f32[1,2048]{1,0:T(1,128)S(1)}, f32[1,2048]{1,0:T(1,128)S(1)}, f32[1,2048]{1,0:T(1,128)S(1)}, f32[1,2048...) fusion(f32[1,2048]{1,0:T(1,128)S(1)} %get-tuple-element.135, ...), kind=kLoop, calls=%fused_computation.313 | loop fusion | flops 186368 | bytes 163924 | tf_op jit(solution)/shard_map/add | solution.py:52
  41.3 13.6 %multiply_add_fusion.15 = (f32[1,2048]{1,0:T(1,128)S(1)}, f32[1,2048]{1,0:T(1,128)S(1)}, f32[1,2048]{1,0:T(1,128)S(1)}, f32[1,2048]{1,0:T(1,128)S(1)}, f32[1,204...) fusion(f32[1,2048]{1,0:T(1,128)S(1)} %get-tuple-element.135, f32[1,2048]{1,0:T(1,128)S(1)} %get-tuple-element.134, ...), kind=kLoop, calls=%fused_computation.321 | loop fusion | flops 182272 | bytes 155732 | tf_op jit(solution)/shard_map/add | solution.py:52
  54.9 13.3 %multiply_add_fusion.8 = f32[1,2048]{1,0:T(1,128)S(1)} fusion(f32[1,2048]{1,0:T(1,128)S(1)} %get-tuple-element.148, f32[1,2048]{1,0:T(1,128)S(1)} %get-tuple-element.147, f32[1,2048]{1,0:T(1,128)S(1)} %get-tuple-element.146, f32[1,2048]{1,0:T(1,128)S(1)} %get-tuple-element.145, f32[1,2048]{1,0:T(1,128)S(1)} %get-tuple-element.144, ...), kind=kLoop, calls=%fused_computation.314 | loop fusion | flops 157696 | bytes 57428 | tf_op jit(solution)/shard_map/add | solution.py:52
  68.2 13.3 %multiply_add_fusion.16 = f32[1,2048]{1,0:T(1,128)S(1)} fusion(f32[1,2048]{1,0:T(1,128)S(1)} %get-tuple-element.148, f32[1,2048]{1,0:T(1,128)S(1)} %get-tuple-element.147, f32[1,2048]{1,0:T(1,128)S(1)} %get-tuple-element.146, f32[1,2048]{1,0:T(1,128)S(1)} %get-tuple-element.145, f32[1,2048]{1,0:T(1,128)S(1)} %get-tuple-element.144, ...), kind=kLoop, calls=%fused_computation.322 | loop fusion | flops 157696 | bytes 106580 | tf_op jit(solution)/shard_map/add | solution.py:52
  81.5 13.3 %multiply_add_fusion.17 = f32[1,2048]{1,0:T(1,128)S(1)} fusion(f32[1,2048]{1,0:T(1,128)S(1)} %get-tuple-element.157, f32[1,2048]{1,0:T(1,128)S(1)} %get-tuple-element.156, f32[1,2048]{1,0:T(1,128)S(1)} %get-tuple-element.155, f32[1,2048]{1,0:T(1,128)S(1)} %get-tuple-element.154, f32[1,2048]{1,0:T(1,128)S(1)} %get-tuple-element.153, ...), kind=kLoop, calls=%fused_computation.323 | loop fusion | flops 157696 | bytes 57428 | tf_op jit(solution)/shard_map/add | solution.py:52
  94.8 13.3 %multiply_add_fusion.34 = (f32[1,2048]{1,0:T(1,128)S(1)}, f32[1,2048]{1,0:T(1,128)S(1)}, f32[1,2048]{1,0:T(1,128)S(1)}, f32[1,2048]{1,0:T(1,128)S(1)}, f32[1,204...) fusion(f32[1,2048]{1,0:T(1,128)S(1)} %get-tuple-element.135, ...), kind=kLoop, calls=%fused_computation.340 | loop fusion | flops 174080 | bytes 155732 | tf_op jit(solution)/shard_map/add | solution.py:52
  108.1 13.5 %multiply_add_fusion.24 = (f32[1,2048]{1,0:T(1,128)S(1)}, f32[1,2048]{1,0:T(1,128)S(1)}, f32[1,2048]{1,0:T(1,128)S(1)}, f32[1,2048]{1,0:T(1,128)S(1)}, f32[1,204...) fusion(f32[1,2048]{1,0:T(1,128)S(1)} %get-tuple-element.135, ...), kind=kLoop, calls=%fused_computation.330 | loop fusion | flops 174080 | bytes 139348 | tf_op jit(solution)/shard_map/add | solution.py:52
  121.8 13.3 %multiply_add_fusion.45 = (f32[1,2048]{1,0:T(1,128)S(1)}, f32[1,2048]{1,0:T(1,128)S(1)}, f32[1,2048]{1,0:T(1,128)S(1)}, f32[1,2048]{1,0:T(1,128)S(1)}, f32[1,204...) fusion(f32[1,2048]{1,0:T(1,128)S(1)} %get-tuple-element.135, ...), kind=kLoop, calls=%fused_computation.351 | loop fusion | flops 174080 | bytes 155732 | tf_op jit(solution)/shard_map/add | solution.py:52
  137.8 25.7 %while.13 = (s32[]{:T(128)}, f32[21,512]{0,1:T(8,128)S(1)}, f32[512]{0:T(512)S(1)}, s32[4,4,512]{2,1,0:T(4,128)S(1)}, f32[21,2048]{0,1:T(8,128)S(1)}, /*index=5*/bf16[4,4,512]{2,1,0:T(4,128)(2,1)S(1)}, s32[]{:T(128)}, s32[]{:T(128)}) while((s32[]{:T(128)}, f32[21,512]{0,1:T(8,128)S(1)}, f32[512]{0:T(512)S(1)}, ...), condition=%wide.region_3.4_spmd.clone, body=%wide.region_0.3_spmd.clone.sunk | while | flops 166915 | bytes 790640 | solution.py:123
  137.8 5.5 %gather_fusion = f32[2048,21]{1,0:T(8,128)S(1)} fusion(f32[21,2048]{0,1:T(8,128)S(1)} %get-tuple-element.325, s32[2048]{0:T(1024)S(1)} %broadcast_clamp_fusion.2), kind=kCustom, calls=%fused_computation.clone.clone.1 | custom fusion | bytes 352256 | tf_op jit(solution)/shard_map/while/body/eval_jaxpr/jit(_take)/gather | solution.py:112
  144.2 5.5 %gather_fusion = f32[2048,21]{1,0:T(8,128)S(1)} fusion(f32[21,2048]{0,1:T(8,128)S(1)} %get-tuple-element.325, s32[2048]{0:T(1024)S(1)} %broadcast_clamp_fusion.2), kind=kCustom, calls=%fused_computation.clone.clone.1 | custom fusion | bytes 352256 | tf_op jit(solution)/shard_map/while/body/eval_jaxpr/jit(_take)/gather | solution.py:112
  150.7 5.5 %gather_fusion = f32[2048,21]{1,0:T(8,128)S(1)} fusion(f32[21,2048]{0,1:T(8,128)S(1)} %get-tuple-element.325, s32[2048]{0:T(1024)S(1)} %broadcast_clamp_fusion.2), kind=kCustom, calls=%fused_computation.clone.clone.1 | custom fusion | bytes 352256 | tf_op jit(solution)/shard_map/while/body/eval_jaxpr/jit(_take)/gather | solution.py:112
  157.1 5.5 %gather_fusion = f32[2048,21]{1,0:T(8,128)S(1)} fusion(f32[21,2048]{0,1:T(8,128)S(1)} %get-tuple-element.325, s32[2048]{0:T(1024)S(1)} %broadcast_clamp_fusion.2), kind=kCustom, calls=%fused_computation.clone.clone.1 | custom fusion | bytes 352256 | tf_op jit(solution)/shard_map/while/body/eval_jaxpr/jit(_take)/gather | solution.py:112
  163.5 2.4 scatter_custom_fusion
  166.0 2.4 scatter_custom_fusion.1
  168.6 7.2 %all-reduce = f32[16,1,2,16]{0,2,1,3:T(2,128)S(1)} all-reduce(f32[16,1,2,16]{0,2,1,3:T(2,128)S(1)} %copy.156), channel_id=3, replica_groups=mesh['gx'=8,'gy'=2,'ga'=2] {'ga'}, use_global_device_ids=true, to_apply=%region_7.8.clone | all-reduce | flops 512 | bytes 4096
  177.8 1.3 collective-permute-start.17
  179.1 4.6 %collective-permute-start.18 = (f32[6,16,4,8]{1,3,2,0:T(8,128)S(1)}, f32[6,16,4,8]{1,3,2,0:T(8,128)S(1)}, u32[]{:S(2)}, u32[]{:S(2)}) collective-permute-start(f32[6,16,4,8]{1,3,2,0:T(8,128)S(1)} %pad_maximum_fusion.13), channel_id=1, source_target_pairs={{2,0},{3,1},{6,4},{7,5},{10,8},{11,9},{14,12},{15,13},{18,16},{19,... | collective-permute-start | bytes 36872 | tf_op jit(solution)/shard_map/ppermute | solution.py:38
  186.2 1.3 collective-permute-start.19
  187.5 4.7 %collective-permute-start.20 = (f32[6,16,12,4]{1,3,2,0:T(4,128)S(1)}, f32[6,16,12,4]{1,3,2,0:T(4,128)S(1)}, u32[]{:S(2)}, u32[]{:S(2)}) collective-permute-start(f32[6,16,12,4]{1,3,2,0:T(4,128)S(1)} %get-tuple-element.205), channel_id=1, source_target_pairs={{1,0},{3,2},{5,4},{7,6},{9,8},{11,10},{13,12},{15,14},{17,16},{19,... | collective-permute-start | bytes 55304 | tf_op jit(solution)/shard_map/ppermute | solution.py:38
  197.3 1.3 collective-permute-start.21
  198.6 3.0 collective-permute-start.22
  202.5 4.4 %collective-permute-start.23 = (f32[3,16,4,8]{3,2,1,0:T(4,128)S(1)}, f32[3,16,4,8]{3,2,1,0:T(4,128)S(1)}, u32[]{:S(2)}, u32[]{:S(2)}) collective-permute-start(f32[3,16,4,8]{3,2,1,0:T(4,128)S(1)} %pad_maximum_fusion.14), channel_id=1, source_target_pairs={{2,0},{3,1},{6,4},{7,5},{10,8},{11,9},{14,12},{15,13},{18,16},{19,... | collective-permute-start | bytes 18440 | tf_op jit(solution)/shard_map/ppermute | solution.py:38
  206.9 1.3 collective-permute-start.24
  209.1 4.3 %collective-permute-done.24 = f32[3,16,4,8]{3,2,1,0:T(4,128)S(1)} collective-permute-done((f32[3,16,4,8]{3,2,1,0:T(4,128)S(1)}, f32[3,16,4,8]{3,2,1,0:T(4,128)S(1)}, u32[]{:S(2)}, u32[]{:S(2)}) %collective-permute-start.24) | collective-permute-done | bytes 6176 | tf_op jit(solution)/shard_map/ppermute | solution.py:36
  213.7 4.4 %collective-permute-start.25 = (f32[3,16,12,4]{3,2,1,0:T(8,128)S(1)}, f32[3,16,12,4]{3,2,1,0:T(8,128)S(1)}, u32[]{:S(2)}, u32[]{:S(2)}) collective-permute-start(f32[3,16,12,4]{3,2,1,0:T(8,128)S(1)} %get-tuple-element.202), channel_id=1, source_target_pairs={{1,0},{3,2},{5,4},{7,6},{9,8},{11,10},{13,12},{15,14},{17,16},{19,... | collective-permute-start | bytes 27656 | tf_op jit(solution)/shard_map/ppermute | solution.py:38
  218.1 1.3 collective-permute-start.26
  219.5 6.7 %collective-permute-done.25 = f32[3,16,12,4]{3,2,1,0:T(8,128)S(1)} collective-permute-done((f32[3,16,12,4]{3,2,1,0:T(8,128)S(1)}, f32[3,16,12,4]{3,2,1,0:T(8,128)S(1)}, u32[]{:S(2)}, u32[]{:S(2)}) %collective-permute-start.25) | collective-permute-done | bytes 9248 | tf_op jit(solution)/shard_map/ppermute | solution.py:38
  226.2 4.7 %collective-permute-done.26 = f32[3,16,12,4]{3,2,1,0:T(8,128)S(1)} collective-permute-done((f32[3,16,12,4]{3,2,1,0:T(8,128)S(1)}, f32[3,16,12,4]{3,2,1,0:T(8,128)S(1)}, u32[]{:S(2)}, u32[]{:S(2)}) %collective-permute-start.26) | collective-permute-done | bytes 9248 | tf_op jit(solution)/shard_map/ppermute | solution.py:36
  233.1 3.1 collective-permute-start.1
  236.1 2.0 collective-permute-start.2
  238.1 1.6 collective-permute-start.3
  239.8 2.2 collective-permute-start.5
  242.0 2.5 collective-permute-start.6
  244.6 1.2 collective-permute-start.7
  246.6 2.1 collective-permute-start.9
  248.7 2.1 collective-permute-start.10
  252.2 1.5 collective-permute-start.13
  253.7 2.3 collective-permute-start.14
  256.1 1.3 collective-permute-done.14
  257.9 1.7 slice_reduce_fusion
  260.8 1.3 collective-permute-start.27
  262.1 1.3 collective-permute-start.28
  263.4 2.1 collective-permute-done.28
  265.5 1.3 collective-permute-start.29
  266.8 4.6 %collective-permute-start.30 = (f32[6,16,4,8]{3,2,1,0:T(4,128)S(1)}, f32[6,16,4,8]{3,2,1,0:T(4,128)S(1)}, u32[]{:S(2)}, u32[]{:S(2)}) collective-permute-start(f32[6,16,4,8]{3,2,1,0:T(4,128)S(1)} %pad_maximum_fusion.12), channel_id=1, source_target_pairs={{2,0},{3,1},{6,4},{7,5},{10,8},{11,9},{14,12},{15,13},{18,16},{19,... | collective-permute-start | bytes 36872 | tf_op jit(solution)/shard_map/ppermute | solution.py:38
  271.4 2.0 collective-permute-done.29
  273.4 1.7 collective-permute-done.30
  276.1 1.3 collective-permute-start.31
  277.9 4.5 %collective-permute-start.32 = (f32[6,16,12,4]{1,3,2,0:T(4,128)S(1)}, f32[6,16,12,4]{1,3,2,0:T(4,128)S(1)}, u32[]{:S(2)}, u32[]{:S(2)}) collective-permute-start(f32[6,16,12,4]{1,3,2,0:T(4,128)S(1)} %copy.179), channel_id=1, source_target_pairs={{1,0},{3,2},{5,4},{7,6},{9,8},{11,10},{13,12},{15,14},{17,16},{19,... | collective-permute-start | bytes 55304 | tf_op jit(solution)/shard_map/ppermute | solution.py:38
  282.5 1.5 collective-permute-done.31
  284.6 1.7 collective-permute-done.32
  288.4 1.3 collective-permute-start.33
  289.7 3.1 collective-permute-start.34
  293.6 4.7 %collective-permute-start.35 = (f32[3,16,4,8]{3,2,1,0:T(4,128)S(1)}, f32[3,16,4,8]{3,2,1,0:T(4,128)S(1)}, u32[]{:S(2)}, u32[]{:S(2)}) collective-permute-start(f32[3,16,4,8]{3,2,1,0:T(4,128)S(1)} %pad_maximum_fusion.15), channel_id=1, source_target_pairs={{2,0},{3,1},{6,4},{7,5},{10,8},{11,9},{14,12},{15,13},{18,16},{19,... | collective-permute-start | bytes 18440 | tf_op jit(solution)/shard_map/ppermute | solution.py:38
  298.3 1.3 collective-permute-start.36
  300.5 4.7 %collective-permute-done.36 = f32[3,16,4,8]{3,2,1,0:T(4,128)S(1)} collective-permute-done((f32[3,16,4,8]{3,2,1,0:T(4,128)S(1)}, f32[3,16,4,8]{3,2,1,0:T(4,128)S(1)}, u32[]{:S(2)}, u32[]{:S(2)}) %collective-permute-start.36) | collective-permute-done | bytes 6176 | tf_op jit(solution)/shard_map/ppermute | solution.py:36
  305.5 4.4 %collective-permute-start.37 = (f32[3,16,12,4]{3,2,1,0:T(8,128)S(1)}, f32[3,16,12,4]{3,2,1,0:T(8,128)S(1)}, u32[]{:S(2)}, u32[]{:S(2)}) collective-permute-start(f32[3,16,12,4]{3,2,1,0:T(8,128)S(1)} %get-tuple-element.200), channel_id=1, source_target_pairs={{1,0},{3,2},{5,4},{7,6},{9,8},{11,10},{13,12},{15,14},{17,16},{19,... | collective-permute-start | bytes 27656 | tf_op jit(solution)/shard_map/ppermute | solution.py:38
  309.9 1.3 collective-permute-start.38
  311.4 7.4 %collective-permute-done.37 = f32[3,16,12,4]{3,2,1,0:T(8,128)S(1)} collective-permute-done((f32[3,16,12,4]{3,2,1,0:T(8,128)S(1)}, f32[3,16,12,4]{3,2,1,0:T(8,128)S(1)}, u32[]{:S(2)}, u32[]{:S(2)}) %collective-permute-start.37) | collective-permute-done | bytes 9248 | tf_op jit(solution)/shard_map/ppermute | solution.py:38
  318.8 4.1 %collective-permute-done.38 = f32[3,16,12,4]{3,2,1,0:T(8,128)S(1)} collective-permute-done((f32[3,16,12,4]{3,2,1,0:T(8,128)S(1)}, f32[3,16,12,4]{3,2,1,0:T(8,128)S(1)}, u32[]{:S(2)}, u32[]{:S(2)}) %collective-permute-start.38) | collective-permute-done | bytes 9248 | tf_op jit(solution)/shard_map/ppermute | solution.py:36
  (188 shorter events, 34.7 us)
Async XLA Ops:
  7.2 224.6 %reduce-scatter.2.cloned.1.call-start = ((), (), s32[]{:S(2)}) async-start(), calls=%async_computation.1 | async-start | bytes 393216 | tf_op jit(solution)/shard_map/reduce_scatter | solution.py:214
  8.3 3.1 copy-start.3
  8.3 169.4 %collective-permute-start.15 = (f32[6,4,4,8]{1,3,2,0:T(8,128)S(1)}, f32[6,4,4,8]{1,3,2,0:T(8,128)S(1)}, u32[]{:S(2)}, u32[]{:S(2)}) collective-permute-start(f32[6,4,4,8]{1,3,2,0:T(8,128)S(1)} %get-tuple-element.229), channel_id=1, source_target_pairs={{0,4},{4,8},{8,12},{12,16},{16,20},{20,24},{24,28},{1,5},{5,9},{9,... | collective-permute-start | bytes 9224 | tf_op jit(solution)/shard_map/ppermute | solution.py:36
  10.0 167.6 %collective-permute-start.16 = (f32[6,4,4,8]{1,3,2,0:T(8,128)S(1)}, f32[6,4,4,8]{1,3,2,0:T(8,128)S(1)}, u32[]{:S(2)}, u32[]{:S(2)}) collective-permute-start(f32[6,4,4,8]{1,3,2,0:T(8,128)S(1)} %get-tuple-element.230), channel_id=1, source_target_pairs={{4,0},{8,4},{12,8},{16,12},{20,16},{24,20},{28,24},{5,1},{9,5},{13... | collective-permute-start | bytes 9224 | tf_op jit(solution)/shard_map/ppermute | solution.py:38
  12.7 0.8 copy-start.4
  136.2 0.8 copy-start.7
  137.0 0.7 copy-start.8
  137.8 25.7 %copy-start.10 = (s32[1,1,512]{2,1,0:T(1,128)S(1)}, s32[1,1,512]{2,1,0:T(1,128)}, u32[]{:S(2)}) copy-start(s32[1,1,512]{2,1,0:T(1,128)} %param.14) | copy-start | bytes 6148
  175.7 0.7 copy-start.11
  177.8 7.1 %collective-permute-start.17 = (f32[6,16,4,8]{1,3,2,0:T(8,128)S(1)}, f32[6,16,4,8]{1,3,2,0:T(8,128)S(1)}, u32[]{:S(2)}, u32[]{:S(2)}) collective-permute-start(f32[6,16,4,8]{1,3,2,0:T(8,128)S(1)} %pad_maximum_fusion.13), channel_id=1, source_target_pairs={{0,2},{1,3},{4,6},{5,7},{8,10},{9,11},{12,14},{13,15},{16,18},{17,... | collective-permute-start | bytes 36872 | tf_op jit(solution)/shard_map/ppermute | solution.py:36
  179.1 6.9 %collective-permute-start.18 = (f32[6,16,4,8]{1,3,2,0:T(8,128)S(1)}, f32[6,16,4,8]{1,3,2,0:T(8,128)S(1)}, u32[]{:S(2)}, u32[]{:S(2)}) collective-permute-start(f32[6,16,4,8]{1,3,2,0:T(8,128)S(1)} %pad_maximum_fusion.13), channel_id=1, source_target_pairs={{2,0},{3,1},{6,4},{7,5},{10,8},{11,9},{14,12},{15,13},{18,16},{19,... | collective-permute-start | bytes 36872 | tf_op jit(solution)/shard_map/ppermute | solution.py:38
  186.2 7.0 %collective-permute-start.19 = (f32[6,16,12,4]{1,3,2,0:T(4,128)S(1)}, f32[6,16,12,4]{1,3,2,0:T(4,128)S(1)}, u32[]{:S(2)}, u32[]{:S(2)}) collective-permute-start(f32[6,16,12,4]{1,3,2,0:T(4,128)S(1)} %get-tuple-element.204), channel_id=1, source_target_pairs={{0,1},{2,3},{4,5},{6,7},{8,9},{10,11},{12,13},{14,15},{16,17},{18,... | collective-permute-start | bytes 55304 | tf_op jit(solution)/shard_map/ppermute | solution.py:36
  187.5 7.2 %collective-permute-start.20 = (f32[6,16,12,4]{1,3,2,0:T(4,128)S(1)}, f32[6,16,12,4]{1,3,2,0:T(4,128)S(1)}, u32[]{:S(2)}, u32[]{:S(2)}) collective-permute-start(f32[6,16,12,4]{1,3,2,0:T(4,128)S(1)} %get-tuple-element.205), channel_id=1, source_target_pairs={{1,0},{3,2},{5,4},{7,6},{9,8},{11,10},{13,12},{15,14},{17,16},{19,... | collective-permute-start | bytes 55304 | tf_op jit(solution)/shard_map/ppermute | solution.py:38
  195.8 0.7 copy-start.5
  195.8 0.8 copy-start.6
  197.3 4.5 %collective-permute-start.21 = (f32[3,4,4,8]{3,2,1,0:T(4,128)S(1)}, f32[3,4,4,8]{3,2,1,0:T(4,128)S(1)}, u32[]{:S(2)}, u32[]{:S(2)}) collective-permute-start(f32[3,4,4,8]{3,2,1,0:T(4,128)S(1)} %get-tuple-element.236), channel_id=1, source_target_pairs={{4,0},{8,4},{12,8},{16,12},{20,16},{24,20},{28,24},{5,1},{9,5},{13... | collective-permute-start | bytes 4616 | tf_op jit(solution)/shard_map/ppermute | solution.py:38
  198.6 3.9 %collective-permute-start.22 = (f32[3,4,4,8]{3,2,1,0:T(4,128)S(1)}, f32[3,4,4,8]{3,2,1,0:T(4,128)S(1)}, u32[]{:S(2)}, u32[]{:S(2)}) collective-permute-start(f32[3,4,4,8]{3,2,1,0:T(4,128)S(1)} %get-tuple-element.235), channel_id=1, source_target_pairs={{0,4},{4,8},{8,12},{12,16},{16,20},{20,24},{24,28},{1,5},{5,9},{9,... | collective-permute-start | bytes 4616 | tf_op jit(solution)/shard_map/ppermute | solution.py:36
  202.5 6.6 %collective-permute-start.23 = (f32[3,16,4,8]{3,2,1,0:T(4,128)S(1)}, f32[3,16,4,8]{3,2,1,0:T(4,128)S(1)}, u32[]{:S(2)}, u32[]{:S(2)}) collective-permute-start(f32[3,16,4,8]{3,2,1,0:T(4,128)S(1)} %pad_maximum_fusion.14), channel_id=1, source_target_pairs={{2,0},{3,1},{6,4},{7,5},{10,8},{11,9},{14,12},{15,13},{18,16},{19,... | collective-permute-start | bytes 18440 | tf_op jit(solution)/shard_map/ppermute | solution.py:38
  206.9 6.5 %collective-permute-start.24 = (f32[3,16,4,8]{3,2,1,0:T(4,128)S(1)}, f32[3,16,4,8]{3,2,1,0:T(4,128)S(1)}, u32[]{:S(2)}, u32[]{:S(2)}) collective-permute-start(f32[3,16,4,8]{3,2,1,0:T(4,128)S(1)} %pad_maximum_fusion.14), channel_id=1, source_target_pairs={{0,2},{1,3},{4,6},{5,7},{8,10},{9,11},{12,14},{13,15},{16,18},{17,... | collective-permute-start | bytes 18440 | tf_op jit(solution)/shard_map/ppermute | solution.py:36
  213.7 12.6 %collective-permute-start.25 = (f32[3,16,12,4]{3,2,1,0:T(8,128)S(1)}, f32[3,16,12,4]{3,2,1,0:T(8,128)S(1)}, u32[]{:S(2)}, u32[]{:S(2)}) collective-permute-start(f32[3,16,12,4]{3,2,1,0:T(8,128)S(1)} %get-tuple-element.202), channel_id=1, source_target_pairs={{1,0},{3,2},{5,4},{7,6},{9,8},{11,10},{13,12},{15,14},{17,16},{19,... | collective-permute-start | bytes 27656 | tf_op jit(solution)/shard_map/ppermute | solution.py:38
  218.1 12.8 %collective-permute-start.26 = (f32[3,16,12,4]{3,2,1,0:T(8,128)S(1)}, f32[3,16,12,4]{3,2,1,0:T(8,128)S(1)}, u32[]{:S(2)}, u32[]{:S(2)}) collective-permute-start(f32[3,16,12,4]{3,2,1,0:T(8,128)S(1)} %get-tuple-element.203), channel_id=1, source_target_pairs={{0,1},{2,3},{4,5},{6,7},{8,9},{10,11},{12,13},{14,15},{16,17},{18,... | collective-permute-start | bytes 27656 | tf_op jit(solution)/shard_map/ppermute | solution.py:36
  232.9 6.9 %collective-permute-start = (f32[21,1,1,2,8]{0,4,3,2,1:T(8,128)S(1)}, f32[21,1,1,2,8]{0,4,3,2,1:T(8,128)S(1)}, u32[]{:S(2)}, u32[]{:S(2)}) collective-permute-start(f32[21,1,1,2,8]{0,4,3,2,1:T(8,128)S(1)} %get-tuple-element.226), channel_id=1, source_target_pairs={{0,2},{2,4},{4,6},{6,8},{8,10},{10,12},{12,14},{14,16},{16,18},{18... | collective-permute-start | bytes 4040 | tf_op jit(solution)/shard_map/ppermute | solution.py:224
  233.1 9.0 %collective-permute-start.1 = (f32[21,1,1,2,8]{0,4,3,2,1:T(8,128)S(1)}, f32[21,1,1,2,8]{0,4,3,2,1:T(8,128)S(1)}, u32[]{:S(2)}, u32[]{:S(2)}) collective-permute-start(f32[21,1,1,2,8]{0,4,3,2,1:T(8,128)S(1)} %get-tuple-element.225), channel_id=1, source_target_pairs={{0,4},{2,6},{4,8},{6,10},{8,12},{10,14},{12,16},{14,18},{16,20},{1... | collective-permute-start | bytes 4040 | tf_op jit(solution)/shard_map/ppermute | solution.py:224
  236.1 8.4 %collective-permute-start.2 = (f32[21,1,1,2,8]{0,4,3,2,1:T(8,128)S(1)}, f32[21,1,1,2,8]{0,4,3,2,1:T(8,128)S(1)}, u32[]{:S(2)}, u32[]{:S(2)}) collective-permute-start(f32[21,1,1,2,8]{0,4,3,2,1:T(8,128)S(1)} %get-tuple-element.224), channel_id=1, source_target_pairs={{0,6},{2,8},{4,10},{6,12},{8,14},{10,16},{12,18},{14,20},{16,22},{... | collective-permute-start | bytes 4040 | tf_op jit(solution)/shard_map/ppermute | solution.py:224
  238.1 7.7 %collective-permute-start.3 = (f32[21,1,1,2,8]{0,4,3,2,1:T(8,128)S(1)}, f32[21,1,1,2,8]{0,4,3,2,1:T(8,128)S(1)}, u32[]{:S(2)}, u32[]{:S(2)}) collective-permute-start(f32[21,1,1,2,8]{0,4,3,2,1:T(8,128)S(1)} %get-tuple-element.223), channel_id=1, source_target_pairs={{0,8},{2,10},{4,12},{6,14},{8,16},{10,18},{12,20},{14,22},{16,24},... | collective-permute-start | bytes 4040 | tf_op jit(solution)/shard_map/ppermute | solution.py:224
  239.7 6.8 %collective-permute-start.4 = (f32[21,1,1,2,8]{0,4,3,2,1:T(8,128)S(1)}, f32[21,1,1,2,8]{0,4,3,2,1:T(8,128)S(1)}, u32[]{:S(2)}, u32[]{:S(2)}) collective-permute-start(f32[21,1,1,2,8]{0,4,3,2,1:T(8,128)S(1)} %get-tuple-element.222), channel_id=1, source_target_pairs={{0,10},{2,12},{4,14},{6,16},{8,18},{10,20},{12,22},{14,24},{16,26}... | collective-permute-start | bytes 4040 | tf_op jit(solution)/shard_map/ppermute | solution.py:224
  239.8 8.9 %collective-permute-start.5 = (f32[21,1,1,2,8]{0,4,3,2,1:T(8,128)S(1)}, f32[21,1,1,2,8]{0,4,3,2,1:T(8,128)S(1)}, u32[]{:S(2)}, u32[]{:S(2)}) collective-permute-start(f32[21,1,1,2,8]{0,4,3,2,1:T(8,128)S(1)} %get-tuple-element.221), channel_id=1, source_target_pairs={{0,12},{2,14},{4,16},{6,18},{8,20},{10,22},{12,24},{14,26},{16,28}... | collective-permute-start | bytes 4040 | tf_op jit(solution)/shard_map/ppermute | solution.py:224
  242.0 8.7 %collective-permute-start.6 = (f32[21,1,1,2,8]{0,4,3,2,1:T(8,128)S(1)}, f32[21,1,1,2,8]{0,4,3,2,1:T(8,128)S(1)}, u32[]{:S(2)}, u32[]{:S(2)}) collective-permute-start(f32[21,1,1,2,8]{0,4,3,2,1:T(8,128)S(1)} %get-tuple-element.220), channel_id=1, source_target_pairs={{0,14},{2,16},{4,18},{6,20},{8,22},{10,24},{12,26},{14,28},{16,30}... | collective-permute-start | bytes 4040 | tf_op jit(solution)/shard_map/ppermute | solution.py:224
  244.6 6.8 %collective-permute-start.7 = (f32[21,1,1,2,8]{0,4,3,2,1:T(8,128)S(1)}, f32[21,1,1,2,8]{0,4,3,2,1:T(8,128)S(1)}, u32[]{:S(2)}, u32[]{:S(2)}) collective-permute-start(f32[21,1,1,2,8]{0,4,3,2,1:T(8,128)S(1)} %get-tuple-element.219), channel_id=1, source_target_pairs={{0,16},{2,18},{4,20},{6,22},{8,24},{10,26},{12,28},{14,30},{16,0},... | collective-permute-start | bytes 4040 | tf_op jit(solution)/shard_map/ppermute | solution.py:224
  245.8 6.4 %collective-permute-start.8 = (f32[21,1,1,2,8]{0,4,3,2,1:T(8,128)S(1)}, f32[21,1,1,2,8]{0,4,3,2,1:T(8,128)S(1)}, u32[]{:S(2)}, u32[]{:S(2)}) collective-permute-start(f32[21,1,1,2,8]{0,4,3,2,1:T(8,128)S(1)} %get-tuple-element.218), channel_id=1, source_target_pairs={{0,18},{2,20},{4,22},{6,24},{8,26},{10,28},{12,30},{14,0},{16,2},{... | collective-permute-start | bytes 4040 | tf_op jit(solution)/shard_map/ppermute | solution.py:224
  246.6 7.1 %collective-permute-start.9 = (f32[21,1,1,2,8]{0,4,3,2,1:T(8,128)S(1)}, f32[21,1,1,2,8]{0,4,3,2,1:T(8,128)S(1)}, u32[]{:S(2)}, u32[]{:S(2)}) collective-permute-start(f32[21,1,1,2,8]{0,4,3,2,1:T(8,128)S(1)} %get-tuple-element.217), channel_id=1, source_target_pairs={{0,20},{2,22},{4,24},{6,26},{8,28},{10,30},{12,0},{14,2},{16,4},{1... | collective-permute-start | bytes 4040 | tf_op jit(solution)/shard_map/ppermute | solution.py:224
  248.7 7.3 %collective-permute-start.10 = (f32[21,1,1,2,8]{0,4,3,2,1:T(8,128)S(1)}, f32[21,1,1,2,8]{0,4,3,2,1:T(8,128)S(1)}, u32[]{:S(2)}, u32[]{:S(2)}) collective-permute-start(f32[21,1,1,2,8]{0,4,3,2,1:T(8,128)S(1)} %get-tuple-element.216), channel_id=1, source_target_pairs={{0,22},{2,24},{4,26},{6,28},{8,30},{10,0},{12,2},{14,4},{16,6},{18... | collective-permute-start | bytes 4040 | tf_op jit(solution)/shard_map/ppermute | solution.py:224
  250.8 5.2 %collective-permute-start.11 = (f32[21,1,1,2,8]{0,4,3,2,1:T(8,128)S(1)}, f32[21,1,1,2,8]{0,4,3,2,1:T(8,128)S(1)}, u32[]{:S(2)}, u32[]{:S(2)}) collective-permute-start(f32[21,1,1,2,8]{0,4,3,2,1:T(8,128)S(1)} %get-tuple-element.215), channel_id=1, source_target_pairs={{0,24},{2,26},{4,28},{6,30},{8,0},{10,2},{12,4},{14,6},{16,8},{18,... | collective-permute-start | bytes 4040 | tf_op jit(solution)/shard_map/ppermute | solution.py:224
  251.4 4.6 %collective-permute-start.12 = (f32[21,1,1,2,8]{0,4,3,2,1:T(8,128)S(1)}, f32[21,1,1,2,8]{0,4,3,2,1:T(8,128)S(1)}, u32[]{:S(2)}, u32[]{:S(2)}) collective-permute-start(f32[21,1,1,2,8]{0,4,3,2,1:T(8,128)S(1)} %get-tuple-element.214), channel_id=1, source_target_pairs={{0,26},{2,28},{4,30},{6,0},{8,2},{10,4},{12,6},{14,8},{16,10},{18,... | collective-permute-start | bytes 4040 | tf_op jit(solution)/shard_map/ppermute | solution.py:224
  252.2 3.9 %collective-permute-start.13 = (f32[21,1,1,2,8]{0,4,3,2,1:T(8,128)S(1)}, f32[21,1,1,2,8]{0,4,3,2,1:T(8,128)S(1)}, u32[]{:S(2)}, u32[]{:S(2)}) collective-permute-start(f32[21,1,1,2,8]{0,4,3,2,1:T(8,128)S(1)} %get-tuple-element.213), channel_id=1, source_target_pairs={{0,28},{2,30},{4,0},{6,2},{8,4},{10,6},{12,8},{14,10},{16,12},{18,... | collective-permute-start | bytes 4040 | tf_op jit(solution)/shard_map/ppermute | solution.py:224
  253.7 3.7 %collective-permute-start.14 = (f32[21,1,1,2,8]{0,4,3,2,1:T(8,128)S(1)}, f32[21,1,1,2,8]{0,4,3,2,1:T(8,128)S(1)}, u32[]{:S(2)}, u32[]{:S(2)}) collective-permute-start(f32[21,1,1,2,8]{0,4,3,2,1:T(8,128)S(1)} %get-tuple-element.212), channel_id=1, source_target_pairs={{0,30},{2,0},{4,2},{6,4},{8,6},{10,8},{12,10},{14,12},{16,14},{18,... | collective-permute-start | bytes 4040 | tf_op jit(solution)/shard_map/ppermute | solution.py:224
  257.9 1.7 copy-start
  259.6 0.9 copy-start.2
  260.8 2.6 collective-permute-start.27
  262.1 3.4 %collective-permute-start.28 = (f32[6,4,4,8]{3,2,1,0:T(4,128)S(1)}, f32[6,4,4,8]{3,2,1,0:T(4,128)S(1)}, u32[]{:S(2)}, u32[]{:S(2)}) collective-permute-start(f32[6,4,4,8]{3,2,1,0:T(4,128)S(1)} %get-tuple-element.228), channel_id=1, source_target_pairs={{4,0},{8,4},{12,8},{16,12},{20,16},{24,20},{28,24},{5,1},{9,5},{13... | collective-permute-start | bytes 9224 | tf_op jit(solution)/shard_map/ppermute | solution.py:38
  265.5 7.9 %collective-permute-start.29 = (f32[6,16,4,8]{3,2,1,0:T(4,128)S(1)}, f32[6,16,4,8]{3,2,1,0:T(4,128)S(1)}, u32[]{:S(2)}, u32[]{:S(2)}) collective-permute-start(f32[6,16,4,8]{3,2,1,0:T(4,128)S(1)} %pad_maximum_fusion.12), channel_id=1, source_target_pairs={{0,2},{1,3},{4,6},{5,7},{8,10},{9,11},{12,14},{13,15},{16,18},{17,... | collective-permute-start | bytes 36872 | tf_op jit(solution)/shard_map/ppermute | solution.py:36
  266.8 8.3 %collective-permute-start.30 = (f32[6,16,4,8]{3,2,1,0:T(4,128)S(1)}, f32[6,16,4,8]{3,2,1,0:T(4,128)S(1)}, u32[]{:S(2)}, u32[]{:S(2)}) collective-permute-start(f32[6,16,4,8]{3,2,1,0:T(4,128)S(1)} %pad_maximum_fusion.12), channel_id=1, source_target_pairs={{2,0},{3,1},{6,4},{7,5},{10,8},{11,9},{14,12},{15,13},{18,16},{19,... | collective-permute-start | bytes 36872 | tf_op jit(solution)/shard_map/ppermute | solution.py:38
  276.1 7.9 %collective-permute-start.31 = (f32[6,16,12,4]{1,3,2,0:T(4,128)S(1)}, f32[6,16,12,4]{1,3,2,0:T(4,128)S(1)}, u32[]{:S(2)}, u32[]{:S(2)}) collective-permute-start(f32[6,16,12,4]{1,3,2,0:T(4,128)S(1)} %copy.178), channel_id=1, source_target_pairs={{0,1},{2,3},{4,5},{6,7},{8,9},{10,11},{12,13},{14,15},{16,17},{18,... | collective-permute-start | bytes 55304 | tf_op jit(solution)/shard_map/ppermute | solution.py:36
  277.9 8.4 %collective-permute-start.32 = (f32[6,16,12,4]{1,3,2,0:T(4,128)S(1)}, f32[6,16,12,4]{1,3,2,0:T(4,128)S(1)}, u32[]{:S(2)}, u32[]{:S(2)}) collective-permute-start(f32[6,16,12,4]{1,3,2,0:T(4,128)S(1)} %copy.179), channel_id=1, source_target_pairs={{1,0},{3,2},{5,4},{7,6},{9,8},{11,10},{13,12},{15,14},{17,16},{19,... | collective-permute-start | bytes 55304 | tf_op jit(solution)/shard_map/ppermute | solution.py:38
  288.3 34.6 %copy-start.1 = (f32[3,8,4,8]{3,2,1,0:T(4,128)}, f32[3,8,4,8]{3,2,1,0:T(4,128)S(1)}, u32[]{:S(2)}) copy-start(f32[3,8,4,8]{3,2,1,0:T(4,128)S(1)} %divide_add_fusion) | copy-start | bytes 9220
  288.4 4.4 %collective-permute-start.33 = (f32[3,4,4,8]{3,2,1,0:T(4,128)S(1)}, f32[3,4,4,8]{3,2,1,0:T(4,128)S(1)}, u32[]{:S(2)}, u32[]{:S(2)}) collective-permute-start(f32[3,4,4,8]{3,2,1,0:T(4,128)S(1)} %get-tuple-element.234), channel_id=1, source_target_pairs={{4,0},{8,4},{12,8},{16,12},{20,16},{24,20},{28,24},{5,1},{9,5},{13... | collective-permute-start | bytes 4616 | tf_op jit(solution)/shard_map/ppermute | solution.py:38
  289.7 3.9 %collective-permute-start.34 = (f32[3,4,4,8]{3,2,1,0:T(4,128)S(1)}, f32[3,4,4,8]{3,2,1,0:T(4,128)S(1)}, u32[]{:S(2)}, u32[]{:S(2)}) collective-permute-start(f32[3,4,4,8]{3,2,1,0:T(4,128)S(1)} %get-tuple-element.233), channel_id=1, source_target_pairs={{0,4},{4,8},{8,12},{12,16},{16,20},{20,24},{24,28},{1,5},{5,9},{9,... | collective-permute-start | bytes 4616 | tf_op jit(solution)/shard_map/ppermute | solution.py:36
  293.6 6.9 %collective-permute-start.35 = (f32[3,16,4,8]{3,2,1,0:T(4,128)S(1)}, f32[3,16,4,8]{3,2,1,0:T(4,128)S(1)}, u32[]{:S(2)}, u32[]{:S(2)}) collective-permute-start(f32[3,16,4,8]{3,2,1,0:T(4,128)S(1)} %pad_maximum_fusion.15), channel_id=1, source_target_pairs={{2,0},{3,1},{6,4},{7,5},{10,8},{11,9},{14,12},{15,13},{18,16},{19,... | collective-permute-start | bytes 18440 | tf_op jit(solution)/shard_map/ppermute | solution.py:38
  298.3 7.0 %collective-permute-start.36 = (f32[3,16,4,8]{3,2,1,0:T(4,128)S(1)}, f32[3,16,4,8]{3,2,1,0:T(4,128)S(1)}, u32[]{:S(2)}, u32[]{:S(2)}) collective-permute-start(f32[3,16,4,8]{3,2,1,0:T(4,128)S(1)} %pad_maximum_fusion.15), channel_id=1, source_target_pairs={{0,2},{1,3},{4,6},{5,7},{8,10},{9,11},{12,14},{13,15},{16,18},{17,... | collective-permute-start | bytes 18440 | tf_op jit(solution)/shard_map/ppermute | solution.py:36
  305.5 13.3 %collective-permute-start.37 = (f32[3,16,12,4]{3,2,1,0:T(8,128)S(1)}, f32[3,16,12,4]{3,2,1,0:T(8,128)S(1)}, u32[]{:S(2)}, u32[]{:S(2)}) collective-permute-start(f32[3,16,12,4]{3,2,1,0:T(8,128)S(1)} %get-tuple-element.200), channel_id=1, source_target_pairs={{1,0},{3,2},{5,4},{7,6},{9,8},{11,10},{13,12},{15,14},{17,16},{19,... | collective-permute-start | bytes 27656 | tf_op jit(solution)/shard_map/ppermute | solution.py:38
  309.9 13.0 %collective-permute-start.38 = (f32[3,16,12,4]{3,2,1,0:T(8,128)S(1)}, f32[3,16,12,4]{3,2,1,0:T(8,128)S(1)}, u32[]{:S(2)}, u32[]{:S(2)}) collective-permute-start(f32[3,16,12,4]{3,2,1,0:T(8,128)S(1)} %get-tuple-element.201), channel_id=1, source_target_pairs={{0,1},{2,3},{4,5},{6,7},{8,9},{10,11},{12,13},{14,15},{16,17},{18,... | collective-permute-start | bytes 27656 | tf_op jit(solution)/shard_map/ppermute | solution.py:36
  324.1 0.6 copy-start.9
Sparse Core Ops, SparseCore 0:
  166.1 14.5 reduce-scatter.1
